TPU v7x, 512 devices: a whole 4x8x8 slice. The times are simulated.
512 devices in a mesh: ctx: 32 (over z, x), head: 16 (over y, core).
Axes of the slice: x: 4, y: 8, z: 8, core: 2. Of those that a mesh axis runs over, the one named last changes fastest.
Arguments:
- queries: bfloat16 [16384, 4096], P(('ctx', 'head')), may hold values from -64 to 64
- keys: bfloat16 [16384, 4096], P(('ctx', 'head')), may hold values from -8 to 8
- values: bfloat16 [16384, 4096], P(('ctx', 'head')), may hold values from -6 to 6
Outputs:
- attended: bfloat16 [16384, 4096], P(('ctx', 'head'))
All inputs are finite; a program needn't handle non-finite values.
Results may differ from a plain program's by a relative error of at most 0.0045.
Values may be sent and summed in bfloat16 or wider, within the bound.
No kernel may reach another device: no remote copies, remote signals or barrier semaphores. Data moves between devices by JAX's collectives and lax.ppermute only.
A program may use at most 64 MiB of HBM per device.

v0:
```python
import jax
import jax.numpy as jnp
from jax import lax
from jax.sharding import PartitionSpec as P

HEAD_SIZE = 128
BLOCK = 256
SUM = 16
BAND_REACH = 1024


def from_behind(value, axis, steps):
    count = lax.axis_size(axis)
    initial, last = (max(0, -steps), min(count, count - steps))
    return lax.ppermute(value, axis, [(source, source + steps) for source in range(initial, last)])


def summary_positions(count):
    ridx = jnp.arange(count, dtype=jnp.int32)
    return ridx // SUM * BLOCK + BLOCK - SUM + ridx % SUM


def band_scores(qblk, kb, qpos, bpos):
    scores = jnp.einsum(
        "qhd,khd->hqk", qblk, kb, preferred_element_type=jnp.float32
    ) * HEAD_SIZE ** (-0.5)
    diff = qpos[:, None] - bpos[None, :]
    band_ok = (bpos[None, :] >= 0) & (diff >= 0) & (diff < BAND_REACH)
    return (jnp.where(band_ok[None], scores, -1e30), band_ok)


def sum_scores(qblk, ks, qpos, spos):
    scores = jnp.einsum(
        "qhd,khd->hqk", qblk, ks, preferred_element_type=jnp.float32
    ) * HEAD_SIZE ** (-0.5)
    sum_ok = qpos[:, None] - spos[None, :] >= BAND_REACH
    return (jnp.where(sum_ok[None], scores, -1e30), sum_ok)


def local(queries, keys, values):
    q_dev, k_dev, v_dev = (
        lax.all_to_all(queries, "head", split_axis=1, concat_axis=0, tiled=True),
        lax.all_to_all(keys, "head", split_axis=1, concat_axis=0, tiled=True),
        lax.all_to_all(values, "head", split_axis=1, concat_axis=0, tiled=True),
    )
    tok_rows = q_dev.shape[0]
    heads_here = q_dev.shape[1] // HEAD_SIZE
    q_all = q_dev.reshape(tok_rows, heads_here, HEAD_SIZE)
    k_all = k_dev.reshape(tok_rows, heads_here, HEAD_SIZE)
    value_rows_all = v_dev.reshape(tok_rows, heads_here, HEAD_SIZE)
    base = lax.axis_index("ctx") * tok_rows
    reach_devs = (BAND_REACH + tok_rows - 1) // tok_rows
    band_k_parts = []
    band_v_parts = []
    for dist in range(reach_devs, 0, -1):
        prev_k, prev_v = from_behind((k_all, value_rows_all), "ctx", dist)
        band_k_parts.append(prev_k)
        band_v_parts.append(prev_v)
    k_band = jnp.concatenate(band_k_parts + [k_all], axis=0)
    v_band = jnp.concatenate(band_v_parts + [value_rows_all], axis=0)
    k_sum = k_all.reshape(tok_rows // BLOCK, BLOCK, heads_here, HEAD_SIZE)[
        :, BLOCK - SUM :
    ].reshape(-1, heads_here, HEAD_SIZE)
    v_sum = value_rows_all.reshape(tok_rows // BLOCK, BLOCK, heads_here, HEAD_SIZE)[
        :, BLOCK - SUM :
    ].reshape(-1, heads_here, HEAD_SIZE)
    query_rows = min(512, tok_rows)
    k_seen, v_seen = (
        lax.all_gather(k_sum, "ctx", axis=0, tiled=True),
        lax.all_gather(v_sum, "ctx", axis=0, tiled=True),
    )
    spos = summary_positions(k_seen.shape[0])
    qpos = base + 0 + jnp.arange(query_rows, dtype=jnp.int32)
    bpos = base + 0 - BAND_REACH + jnp.arange(BAND_REACH + query_rows, dtype=jnp.int32)
    sb, band_ok = band_scores(q_all, k_band, qpos, bpos)
    ss, sum_ok = sum_scores(q_all, k_seen, qpos, spos)
    top = jnp.maximum(jnp.max(sb, axis=-1), jnp.max(ss, axis=-1))
    pb = jnp.where(band_ok[None], jnp.exp(sb - top[..., None]), 0.0)
    ps = jnp.where(sum_ok[None], jnp.exp(ss - top[..., None]), 0.0)
    total = jnp.sum(pb, axis=-1) + jnp.sum(ps, axis=-1)
    numer = jnp.einsum(
        "hqk,khd->hqd", pb.astype(jnp.bfloat16), v_band, preferred_element_type=jnp.float32
    )
    numer = numer + jnp.einsum(
        "hqk,khd->hqd", ps.astype(jnp.bfloat16), v_seen, preferred_element_type=jnp.float32
    )
    outputs = (numer / total[..., None]).astype(jnp.bfloat16)
    local_out = jnp.transpose(outputs, (1, 0, 2)).reshape(tok_rows, heads_here * HEAD_SIZE)
    return lax.all_to_all(local_out, "head", split_axis=0, concat_axis=1, tiled=True)


def solution(mesh):
    placed = (P(("ctx", "head"), None), P(("ctx", "head"), None), P(("ctx", "head"), None))
    return jax.shard_map(
        local, mesh=mesh, in_specs=placed, out_specs=P(("ctx", "head"), None), check_vma=False
    )
```

profile of v0, /device:TPU:1, one launch (start us, length us, event | category | flops | bytes accessed | tf_op | source)
XLA Modules:
  0.0 202.9 jit_solution(5113818668140750158)
XLA Ops:
  0.0 1.7 copy.54
  1.7 10.2 %all-to-all-start = ((bf16[32,16,256]{2,0,1:T(8,128)(2,1)}), bf16[32,16,256]{2,0,1:T(8,128)(2,1)S(1)}, u32[]{:S(2)}, u32[]{:S(2)}) async-start(bf16[32,16,256]{2,0,1:T(8,128)(2,1)} %bitcast.48), calls=%async_computation | async-start | bytes 524288 | tf_op jit(solution)/shard_map/all_to_all | solution.py:43
  11.9 1.7 copy.52
  13.5 10.2 %all-to-all-done = bf16[32,16,256]{2,0,1:T(8,128)(2,1)S(1)} async-done(((bf16[32,16,256]{2,0,1:T(8,128)(2,1)}), bf16[32,16,256]{2,0,1:T(8,128)(2,1)S(1)}, u32[]{:S(2)}, u32[]{:S(2)}) %all-to-all-start) | async-done | bytes 262176 | tf_op jit(solution)/shard_map/all_to_all | solution.py:43
  23.7 3.4 %all-to-all-start.2 = ((bf16[32,16,256]{2,0,1:T(8,128)(2,1)}), bf16[32,16,256]{2,0,1:T(8,128)(2,1)S(1)}, u32[]{:S(2)}, u32[]{:S(2)}) async-start(bf16[32,16,256]{2,0,1:T(8,128)(2,1)} %bitcast.46), calls=%async_computation.2 | async-start | bytes 524288 | tf_op jit(solution)/shard_map/all_to_all | solution.py:44
  27.2 1.7 copy.53
  28.9 0.4 subtract_compare_fusion.2
  29.3 8.9 %all-to-all-done.2 = bf16[32,16,256]{2,0,1:T(8,128)(2,1)S(1)} async-done(((bf16[32,16,256]{2,0,1:T(8,128)(2,1)}), bf16[32,16,256]{2,0,1:T(8,128)(2,1)S(1)}, u32[]{:S(2)}, u32[]{:S(2)}) %all-to-all-start.2) | async-done | bytes 262176 | tf_op jit(solution)/shard_map/all_to_all | solution.py:44
  38.2 3.4 %all-to-all-start.1 = ((bf16[32,16,256]{2,0,1:T(8,128)(2,1)}), bf16[32,16,256]{2,0,1:T(8,128)(2,1)S(1)}, u32[]{:S(2)}, u32[]{:S(2)}) async-start(bf16[32,16,256]{2,0,1:T(8,128)(2,1)} %bitcast.47), calls=%async_computation.1 | async-start | bytes 524288 | tf_op jit(solution)/shard_map/all_to_all | solution.py:42
  41.6 1.3 fusion.7
  42.9 0.1 reshape.152
  43.0 3.7 %collective-permute-start = (bf16[512,2,128]{2,0,1:T(8,128)(2,1)S(1)}, bf16[512,2,128]{2,0,1:T(8,128)(2,1)}, u32[]{:S(2)}, u32[]{:S(2)}) collective-permute-start(bf16[512,2,128]{2,0,1:T(8,128)(2,1)S(1)} %copy.21), channel_id=1, source_target_pairs={{0,32},{16,48},{32,64},{48,80},{64,96},{80,112},{96,128},{112,144}... | collective-permute-start | bytes 786440 | tf_op jit(solution)/shard_map/ppermute | solution.py:15
  46.7 2.9 %collective-permute-start.1 = (bf16[512,2,128]{2,0,1:T(8,128)(2,1)S(1)}, bf16[512,2,128]{2,0,1:T(8,128)(2,1)}, u32[]{:S(2)}, u32[]{:S(2)}) collective-permute-start(bf16[512,2,128]{2,0,1:T(8,128)(2,1)S(1)} %copy.21), channel_id=1, source_target_pairs={{0,16},{16,32},{32,48},{48,64},{64,80},{80,96},{96,112},{112,128},... | collective-permute-start | bytes 786440 | tf_op jit(solution)/shard_map/ppermute | solution.py:15
  49.7 0.1 reshape_reshape.6
  49.7 0.1 reshape_reshape.7
  49.8 0.1 reshape.155
  49.9 4.8 %collective-permute-start.2 = (bf16[512,2,128]{2,0,1:T(8,128)(2,1)S(1)}, bf16[512,2,128]{2,0,1:T(8,128)(2,1)}, u32[]{:S(2)}, u32[]{:S(2)}) collective-permute-start(bf16[512,2,128]{2,0,1:T(8,128)(2,1)S(1)} %copy.29), channel_id=1, source_target_pairs={{0,32},{16,48},{32,64},{48,80},{64,96},{80,112},{96,128},{112,144}... | collective-permute-start | bytes 786440 | tf_op jit(solution)/shard_map/ppermute | solution.py:15
  54.7 3.8 %collective-permute-start.3 = (bf16[512,2,128]{2,0,1:T(8,128)(2,1)S(1)}, bf16[512,2,128]{2,0,1:T(8,128)(2,1)}, u32[]{:S(2)}, u32[]{:S(2)}) collective-permute-start(bf16[512,2,128]{2,0,1:T(8,128)(2,1)S(1)} %copy.29), channel_id=1, source_target_pairs={{0,16},{16,32},{32,48},{48,64},{64,80},{80,96},{96,112},{112,128},... | collective-permute-start | bytes 786440 | tf_op jit(solution)/shard_map/ppermute | solution.py:15
  58.5 0.1 reshape.153
  58.6 52.4 %all_gather.6 = bf16[1024,2,128]{2,0,1:T(8,128)(2,1)S(1)} all-gather(bf16[32,2,128]{2,0,1:T(8,128)(2,1)S(1)} %bitcast.58), channel_id=1, replica_groups=mesh['ctx'=32,'head'=16] {'ctx'}, dimensions={0}, use_global_device_ids=true | all-gather | bytes 540672 | tf_op jit(solution)/shard_map/all_gather | solution.py:69
  111.1 37.2 %all_gather.7 = bf16[1024,2,128]{2,0,1:T(8,128)(2,1)S(1)} all-gather(bf16[32,2,128]{2,0,1:T(8,128)(2,1)S(1)} %bitcast.59), channel_id=1, replica_groups=mesh['ctx'=32,'head'=16] {'ctx'}, dimensions={0}, use_global_device_ids=true | all-gather | bytes 540672 | tf_op jit(solution)/shard_map/all_gather | solution.py:70
  148.2 1.1 fusion.3
  149.3 0.0 collective-permute-done.1
  149.3 2.4 %fusion = (f32[2,512]{1,0:T(2,128)S(1)}, f32[2,1536,512]{2,1,0:T(8,128)S(1)}) fusion(pred[512,1536]{0,1:T(8,128)(4,1)S(1)} %fusion.7, bf16[512,2,128]{2,1,0:T(2,128)(2,1)S(1)} %reshape.153, bf16[512,2,128]{2,0,1:T(8,128)(2,1)S(1)} %copy.21, bf16[512,2,128]{2,0,1:T(8,128)(2,1)} %collective-permute-done.1, bf16[512,2,128]{2,0,1:T(8,128)(2,1)} %collective-permute-done), kind=kOutput, calls=%fused_computation.2 | convolution fusion | flops 409730048 | bytes 8130560 | tf_op jit(solution)/shard_map/qhd,khd->hqk/dot_general | solution.py:24
  151.8 1.7 fusion.1
  153.4 1.6 fusion.11
  155.0 1.5 fusion.9
  156.6 3.6 %fusion.23 = bf16[512,2,128]{2,0,1:T(8,128)(2,1)S(1)} fusion(f32[2,512,128]{2,1,0:T(8,128)S(1)} %fusion.11, f32[2,1536,512]{2,1,0:T(8,128)S(1)} %get-tuple-element.6, f32[2,512]{1,0:T(2,128)S(1)} %max.7, pred[512,1536]{0,1:T(8,128)(4,1)S(1)} %fusion.7, bf16[512,2,128]{2,0,1:T(8,128)(2,1)S(1)} %copy.29, bf16[512,2,128]{2,0,1:T(8,128)(2,1)} %collective-permute-done.3, ...), kind=kOutput, calls=%fused_computation.22 | convolution fusion | flops 413270016 | bytes 8658944 | tf_op jit(solution)/shard_map/hqk,khd->hqd/dot_general | solution.py:81
  160.2 0.3 copy.34
  160.4 0.2 all_to_all.59
  160.6 41.6 %all_to_all.67 = bf16[16,32,256]{2,1,0:T(8,128)(2,1)S(1)} all-to-all(bf16[16,32,256]{2,1,0:T(8,128)(2,1)S(1)} %all_to_all.59), channel_id=1, replica_groups=mesh['ctx'=32,'head'=16] {'head'}, dimensions={0} | all-to-all | bytes 524288 | tf_op jit(solution)/shard_map/all_to_all | solution.py:89
  202.2 0.7 copy.40
  (16 shorter events, 0.2 us)
Async XLA Ops:
  1.7 22.1 %all-to-all-start = ((bf16[32,16,256]{2,0,1:T(8,128)(2,1)}), bf16[32,16,256]{2,0,1:T(8,128)(2,1)S(1)}, u32[]{:S(2)}, u32[]{:S(2)}) async-start(bf16[32,16,256]{2,0,1:T(8,128)(2,1)} %bitcast.48), calls=%async_computation | async-start | bytes 524288 | tf_op jit(solution)/shard_map/all_to_all | solution.py:43
  23.7 14.5 %all-to-all-start.2 = ((bf16[32,16,256]{2,0,1:T(8,128)(2,1)}), bf16[32,16,256]{2,0,1:T(8,128)(2,1)S(1)}, u32[]{:S(2)}, u32[]{:S(2)}) async-start(bf16[32,16,256]{2,0,1:T(8,128)(2,1)} %bitcast.46), calls=%async_computation.2 | async-start | bytes 524288 | tf_op jit(solution)/shard_map/all_to_all | solution.py:44
  38.2 20.3 %all-to-all-start.1 = ((bf16[32,16,256]{2,0,1:T(8,128)(2,1)}), bf16[32,16,256]{2,0,1:T(8,128)(2,1)S(1)}, u32[]{:S(2)}, u32[]{:S(2)}) async-start(bf16[32,16,256]{2,0,1:T(8,128)(2,1)} %bitcast.47), calls=%async_computation.1 | async-start | bytes 524288 | tf_op jit(solution)/shard_map/all_to_all | solution.py:42
  43.0 106.3 %collective-permute-start = (bf16[512,2,128]{2,0,1:T(8,128)(2,1)S(1)}, bf16[512,2,128]{2,0,1:T(8,128)(2,1)}, u32[]{:S(2)}, u32[]{:S(2)}) collective-permute-start(bf16[512,2,128]{2,0,1:T(8,128)(2,1)S(1)} %copy.21), channel_id=1, source_target_pairs={{0,32},{16,48},{32,64},{48,80},{64,96},{80,112},{96,128},{112,144}... | collective-permute-start | bytes 786440 | tf_op jit(solution)/shard_map/ppermute | solution.py:15
  46.7 102.6 %collective-permute-start.1 = (bf16[512,2,128]{2,0,1:T(8,128)(2,1)S(1)}, bf16[512,2,128]{2,0,1:T(8,128)(2,1)}, u32[]{:S(2)}, u32[]{:S(2)}) collective-permute-start(bf16[512,2,128]{2,0,1:T(8,128)(2,1)S(1)} %copy.21), channel_id=1, source_target_pairs={{0,16},{16,32},{32,48},{48,64},{64,80},{80,96},{96,112},{112,128},... | collective-permute-start | bytes 786440 | tf_op jit(solution)/shard_map/ppermute | solution.py:15
  49.9 106.6 %collective-permute-start.2 = (bf16[512,2,128]{2,0,1:T(8,128)(2,1)S(1)}, bf16[512,2,128]{2,0,1:T(8,128)(2,1)}, u32[]{:S(2)}, u32[]{:S(2)}) collective-permute-start(bf16[512,2,128]{2,0,1:T(8,128)(2,1)S(1)} %copy.29), channel_id=1, source_target_pairs={{0,32},{16,48},{32,64},{48,80},{64,96},{80,112},{96,128},{112,144}... | collective-permute-start | bytes 786440 | tf_op jit(solution)/shard_map/ppermute | solution.py:15
  54.7 101.9 %collective-permute-start.3 = (bf16[512,2,128]{2,0,1:T(8,128)(2,1)S(1)}, bf16[512,2,128]{2,0,1:T(8,128)(2,1)}, u32[]{:S(2)}, u32[]{:S(2)}) collective-permute-start(bf16[512,2,128]{2,0,1:T(8,128)(2,1)S(1)} %copy.29), channel_id=1, source_target_pairs={{0,16},{16,32},{32,48},{48,64},{64,80},{80,96},{96,112},{112,128},... | collective-permute-start | bytes 786440 | tf_op jit(solution)/shard_map/ppermute | solution.py:15
where the time goes:
time: 204 us; the launch traced here: 203 us
  blocking collectives  131 us (64%)
  starting transfers between devices  32.3 us (16%)
  waiting for transfers between devices  19.1 us (9%)
  matrix products  8.69 us (4%)
  local copies, waits for them, and re-layouts  6.62 us (3%)
  other arithmetic  4.88 us (2%)
    all_gather x1, blocking collectives, local(): lax.all_gather(k_sum, 'ctx', axis=0, tiled=True)  52.4 us
    all_to_all x1, blocking collectives, local(): lax.all_to_all(local_out, 'head', split_axis=0, concat_axis=1, tiled=True)  41.6 us
    all_gather x1, blocking collectives, local(): lax.all_gather(v_sum, 'ctx', axis=0, tiled=True)  37.2 us
    ppermute x4, starting transfers between devices, from_behind(): lax.ppermute(value, axis, [(source, source + steps) for source in range(i...  15.3 us
    all_to_all x1, starting transfers between devices, local(): lax.all_to_all(keys, 'head', split_axis=1, concat_axis=0, tiled=True)  10.2 us
    all_to_all x1, waiting for transfers between devices, local(): lax.all_to_all(keys, 'head', split_axis=1, concat_axis=0, tiled=True)  10.2 us
    all_to_all x1, waiting for transfers between devices, local(): lax.all_to_all(values, 'head', split_axis=1, concat_axis=0, tiled=True)  8.91 us
  transfers between devices with their start and end apart: 7, of which 2 were waited for; matrix products, arithmetic and copies ran while one was open for 7% of the time, Pallas kernels for 0%

commit v1 on v0

v1 whole, which is shorter than its diff:
```python
import functools

import jax
import jax.numpy as jnp
from jax import lax
from jax.experimental import pallas as pl
from jax.experimental.pallas import tpu as pltpu
from jax.sharding import Mesh
from jax.sharding import PartitionSpec as P

HEAD_SIZE = 128
BLOCK = 256
SUM = 16
BAND_REACH = 1024
AXES = ("z", "x", "y", "core")
PLANE = ("x", "y")
ROWS = 32
HEADS = 32
SPAN = 2 * ROWS
SRC = 32
BACK = BAND_REACH // SPAN
TILE = 8
MASKED = -1e30
VMEM = pl.BlockSpec(memory_space=pltpu.VMEM)


def pack_kernel(k_ref, v_ref, q_ref, out_ref):
    for head in range(HEADS):
        cols = slice(head * HEAD_SIZE, (head + 1) * HEAD_SIZE)
        out_ref[head, 0:ROWS, :] = k_ref[:, cols]
        out_ref[head, ROWS:2 * ROWS, :] = v_ref[:, cols]
        out_ref[head, 2 * ROWS:, :] = q_ref[:, cols]


def unpack_kernel(in_ref, out_ref):
    for head in range(HEADS):
        out_ref[:, head * HEAD_SIZE:(head + 1) * HEAD_SIZE] = in_ref[head]


def attend_kernel(place_ref, own_ref, other_ref, back_ref, back_other_ref, sum_ref, out_ref):
    plane, core = place_ref[0], place_ref[1]
    near = ((back_ref, own_ref, core), (back_other_ref, other_ref, 1 - core))
    log2e = 1.4426950408889634
    scale = HEAD_SIZE ** -0.5 * log2e
    tile_rows = TILE * ROWS

    def rows_at(start, offset):
        r = lax.broadcasted_iota(jnp.int32, (tile_rows, 1), 0)
        return (r // ROWS) * SPAN + r % ROWS + start * SPAN + offset

    def cols_at(count, start, offset):
        c = lax.broadcasted_iota(jnp.int32, (1, count), 1)
        return (c // ROWS) * SPAN + c % ROWS + start * SPAN + offset

    def score(q, k):
        return lax.dot_general(q, k, (((1,), (1,)), ((), ())), preferred_element_type=jnp.float32)

    for tile in range(SRC // TILE):
        first = tile * TILE
        q = own_ref[first:first + TILE, 2 * ROWS:, :].reshape(tile_rows, HEAD_SIZE)
        qpos = rows_at(first, core * ROWS)
        reach = jnp.minimum(BAND_REACH, plane * (SRC * SPAN) + qpos + 1)
        parts = []
        for behind, here, parity in near:
            for start in range(first - BACK, first + TILE, TILE):
                source = here if start >= 0 else behind
                at = start if start >= 0 else start + BACK
                k = source[at:at + TILE, 0:ROWS, :].reshape(tile_rows, HEAD_SIZE)
                v = source[at:at + TILE, ROWS:2 * ROWS, :].reshape(tile_rows, HEAD_SIZE)
                s = score(q, k)
                diff = qpos - cols_at(tile_rows, start, parity * ROWS)
                if start == first:
                    s = jnp.where(diff >= 0, s, MASKED)
                elif start < 0 or start == first - BACK:
                    s = jnp.where(diff < reach, s, MASKED)
                parts.append((s, v))
        k = sum_ref[:, :, 0].reshape(-1, HEAD_SIZE)
        v = sum_ref[:, :, 1].reshape(-1, HEAD_SIZE)
        s = score(q, k)
        c = lax.broadcasted_iota(jnp.int32, (1, s.shape[1]), 1)
        spos = (c // SUM) * BLOCK + BLOCK - SUM + c % SUM
        far = plane * (SRC * SPAN) + qpos - BAND_REACH
        parts.append((jnp.where(spos <= far, s, MASKED), v))

        top = functools.reduce(jnp.maximum, [jnp.max(s, axis=1, keepdims=True) for s, _ in parts])
        total = jnp.zeros((tile_rows, 1), jnp.float32)
        numer = jnp.zeros((tile_rows, HEAD_SIZE), jnp.float32)
        for s, v in parts:
            weight = jnp.exp2((s - top) * scale)
            total = total + jnp.sum(weight, axis=1, keepdims=True)
            numer = numer + jnp.dot(weight.astype(jnp.bfloat16), v, preferred_element_type=jnp.float32)
        out_ref[first:first + TILE] = (numer / total).astype(jnp.bfloat16).reshape(TILE, ROWS, HEAD_SIZE)


def local(queries, keys, values):
    bf16 = jnp.bfloat16
    plane, core = lax.axis_index("z"), lax.axis_index("core")
    packed = pl.pallas_call(
        pack_kernel,
        out_shape=jax.ShapeDtypeStruct((HEADS, 3 * ROWS, HEAD_SIZE), bf16),
        in_specs=[VMEM] * 3,
        out_specs=VMEM,
    )(keys, values, queries)
    own = lax.all_to_all(packed, PLANE, 0, 0, tiled=True)
    swap = [(0, 1), (1, 0)]
    planes = lax.axis_size("z")
    pair = own[:, :2 * ROWS]
    behind = lax.ppermute(pair[SRC - BACK:], "z", [(i, i + 1) for i in range(planes - 1)])
    other = lax.ppermute(pair, "core", swap)
    behind_other = lax.ppermute(behind, "core", swap)
    step = BLOCK // SPAN
    picked = [
        jnp.stack([part[step - 1::step, ROWS - SUM:ROWS], part[step - 1::step, 2 * ROWS - SUM:]], axis=1)
        for part in (pair, other)
    ]
    mine = jnp.where(core == 1, picked[0], picked[1])
    sums = lax.all_to_all(
        jnp.broadcast_to(mine[None], (planes, *mine.shape)), "z", 0, 0, tiled=True
    )
    place = jnp.stack([plane, core]).astype(jnp.int32)
    out = pl.pallas_call(
        attend_kernel,
        out_shape=jax.ShapeDtypeStruct((SRC, ROWS, HEAD_SIZE), bf16),
        in_specs=[pl.BlockSpec(memory_space=pltpu.SMEM)] + [VMEM] * 5,
        out_specs=VMEM,
        compiler_params=pltpu.CompilerParams(vmem_limit_bytes=48 * 2**20),
    )(place, own, other, behind, behind_other, sums)
    back = lax.all_to_all(out, PLANE, 0, 0, tiled=True)
    return pl.pallas_call(
        unpack_kernel,
        out_shape=jax.ShapeDtypeStruct((ROWS, HEADS * HEAD_SIZE), bf16),
        in_specs=[VMEM],
        out_specs=VMEM,
    )(back)


def solution(mesh):
    chips = Mesh(mesh.devices.reshape(8, 4, 8, 2), AXES)
    placed = P(AXES, None)
    return jax.shard_map(
        local, mesh=chips, in_specs=(placed,) * 3, out_specs=placed, check_vma=False
    )
```

time: 204 us -> 95.9 us (0.47)
  the two profiles are of different devices: /device:TPU:1 before, /device:TPU:72 now
where the time goes in v1:
time: 95.9 us; the launch traced here: 95.5 us
  blocking collectives  50.8 us (53%)
  waiting for transfers between devices  17.7 us (18%)
  starting transfers between devices  17.2 us (18%)
  Pallas kernels  8.77 us (9%)
  local copies, waits for them, and re-layouts  0.97 us (1%)
    all_to_all x1, blocking collectives, local(): own = lax.all_to_all(packed, PLANE, 0, 0, tiled=True)  33.3 us
    all_to_all x1, blocking collectives, local(): back = lax.all_to_all(out, PLANE, 0, 0, tiled=True)  17.4 us
    ppermute x1, waiting for transfers between devices, local(): lax.ppermute(pair[SRC - BACK:], 'z', [(i, i + 1) for i in range(planes -...  14.4 us
    all_to_all x1, starting transfers between devices, local(): lax.all_to_all(jnp.broadcast_to(mine[None], (planes, *mine.shape)), 'z',...  9.96 us
    pallas_call x1, Pallas kernels, local(): pl.pallas_call(attend_kernel, out_shape=jax.ShapeDtypeStruct((SRC, ROWS,...  4.94 us
    ppermute x1, starting transfers between devices, local(): lax.ppermute(pair[SRC - BACK:], 'z', [(i, i + 1) for i in range(planes -...  3.37 us
    pallas_call x1, Pallas kernels, local(): pl.pallas_call(pack_kernel, out_shape=jax.ShapeDtypeStruct((HEADS, 3 * RO...  2.14 us
    ppermute x1, starting transfers between devices, local(): other = lax.ppermute(pair, 'core', swap)  1.92 us
  transfers between devices with their start and end apart: 4, of which 3 were waited for; matrix products, arithmetic and copies ran while one was open for 0% of the time, Pallas kernels for 0%

profile of v1, /device:TPU:72, one launch (start us, length us, event | category | flops | bytes accessed | tf_op | source)
XLA Modules:
  0.0 95.5 jit_solution(10123205096646153241)
XLA Ops:
  0.0 2.1 %shard_map.37 = bf16[32,96,128]{2,1,0:T(8,128)(2,1)} custom-call(bf16[32,4096]{1,0:T(8,128)(2,1)} %k_ref.1, bf16[32,4096]{1,0:T(8,128)(2,1)} %v_ref.1, bf16[32,4096]{1,0:T(8,128)(2,1)} %q_ref.1), custom_call_target="tpu_custom_call" | custom-call | tf_op jit(solution)/shard_map/pallas_call | solution.py:98
  2.1 33.3 %all_to_all.15.own_ref = bf16[32,96,128]{2,1,0:T(8,128)(2,1)S(1)} all-to-all(bf16[32,96,128]{2,1,0:T(8,128)(2,1)} %shard_map.37), channel_id=1, replica_groups=mesh['z'=8,'x'=4,'y'=8,'core'=2] {'x','y'}, dimensions={0} | all-to-all | bytes 1572864 | tf_op jit(solution)/shard_map/all_to_all | solution.py:104
  35.5 0.1 slice.25
  35.5 1.9 %collective-permute-start = (bf16[32,64,128]{2,1,0:T(8,128)(2,1)S(1)}, bf16[32,64,128]{2,1,0:T(8,128)(2,1)S(1)}, u32[]{:S(2)}, u32[]{:S(2)}) collective-permute-start(bf16[32,64,128]{2,1,0:T(8,128)(2,1)S(1)} %slice.25), channel_id=1, source_target_pairs={{0,1},{1,0},{2,3},{3,2},{4,5},{5,4},{6,7},{7,6},{8,9},{9,8},{10,11... | collective-permute-start | bytes 1572872 | tf_op jit(solution)/shard_map/ppermute | solution.py:109
  37.5 1.9 %collective-permute-done.other_ref = bf16[32,64,128]{2,1,0:T(8,128)(2,1)S(1)} collective-permute-done((bf16[32,64,128]{2,1,0:T(8,128)(2,1)S(1)}, bf16[32,64,128]{2,1,0:T(8,128)(2,1)S(1)}, u32[]{:S(2)}, u32[]{:S(2)}) %collective-permute-start) | collective-permute-done | bytes 524320 | tf_op jit(solution)/shard_map/ppermute | solution.py:109
  39.4 0.9 broadcast_in_dim.2
  40.3 10.0 %all-to-all-start.1 = ((bf16[8,8,2,16,128]{4,3,2,1,0:T(8,128)(2,1)}), bf16[8,8,2,16,128]{4,3,2,1,0:T(8,128)(2,1)S(1)}, u32[]{:S(2)}, u32[]{:S(2)}) async-start(bf16[8,8,2,16,128]{4,3,2,1,0:T(8,128)(2,1)} %broadcast_in_dim.2), calls=%async_computation.1 | async-start | bytes 1048576 | tf_op jit(solution)/shard_map/all_to_all | solution.py:117
  50.2 3.4 %collective-permute-start.1 = (bf16[16,64,128]{2,1,0:T(8,128)(2,1)S(1)}, bf16[16,64,128]{2,1,0:T(8,128)(2,1)S(1)}, u32[]{:S(2)}, u32[]{:S(2)}) collective-permute-start(bf16[16,64,128]{2,1,0:T(8,128)(2,1)S(1)} %slice.26), channel_id=1, source_target_pairs={{0,64},{64,128},{128,192},{192,256},{256,320},{320,384},{384,448},... | collective-permute-start | bytes 786440 | tf_op jit(solution)/shard_map/ppermute | solution.py:108
  53.6 14.4 %collective-permute-done.1.back_ref = bf16[16,64,128]{2,1,0:T(8,128)(2,1)S(1)} collective-permute-done((bf16[16,64,128]{2,1,0:T(8,128)(2,1)S(1)}, bf16[16,64,128]{2,1,0:T(8,128)(2,1)S(1)}, u32[]{:S(2)}, u32[]{:S(2)}) %collective-permute-start.1) | collective-permute-done | bytes 262176 | tf_op jit(solution)/shard_map/ppermute | solution.py:108
  68.0 1.9 %collective-permute-start.2 = (bf16[16,64,128]{2,1,0:T(8,128)(2,1)S(1)}, bf16[16,64,128]{2,1,0:T(8,128)(2,1)S(1)}, u32[]{:S(2)}, u32[]{:S(2)}) collective-permute-start(bf16[16,64,128]{2,1,0:T(8,128)(2,1)S(1)} %collective-permute-done.1.back_ref), channel_id=1, source_target_pairs={{0,1},{1,0},{2,3},{3,2},{4,5},{5,4},{6,7},{7,6},{8,9},{9,8},{10,11... | collective-permute-start | bytes 786440 | tf_op jit(solution)/shard_map/ppermute | solution.py:110
  69.9 0.1 pad_add_fusion.place_ref
  70.0 1.4 %collective-permute-done.2.back_other_ref = bf16[16,64,128]{2,1,0:T(8,128)(2,1)S(1)} collective-permute-done((bf16[16,64,128]{2,1,0:T(8,128)(2,1)S(1)}, bf16[16,64,128]{2,1,0:T(8,128)(2,1)S(1)}, u32[]{:S(2)}, u32[]{:S(2)}) %collective-permute-start.2) | collective-permute-done | bytes 262176 | tf_op jit(solution)/shard_map/ppermute | solution.py:110
  71.4 0.0 all-to-all-done.1.sum_ref
  71.4 4.9 %shard_map.38 = bf16[32,32,128]{2,1,0:T(8,128)(2,1)S(1)} custom-call(s32[2]{0:T(128)S(1)} %pad_add_fusion.place_ref, bf16[32,96,128]{2,1,0:T(8,128)(2,1)S(1)} %all_to_all.15.own_ref, bf16[32,64,128]{2,1,0:T(8,128)(2,1)S(1)} %collective-permute-done.other_ref, bf16[16,64,128]{2,1,0:T(8,128)(2,1)S(1)} %collective-permute-done.1.back_ref, ...), custom_call_target="tpu_custom_call" | custom-call | tf_op jit(solution)/shard_map/pallas_call | solution.py:121
  76.4 17.4 %all_to_all.16.in_ref = bf16[32,32,128]{2,1,0:T(8,128)(2,1)} all-to-all(bf16[32,32,128]{2,1,0:T(8,128)(2,1)S(1)} %shard_map.38), channel_id=1, replica_groups=mesh['z'=8,'x'=4,'y'=8,'core'=2] {'x','y'}, dimensions={0} | all-to-all | bytes 524288 | tf_op jit(solution)/shard_map/all_to_all | solution.py:128
  93.8 1.7 %shard_map.39 = bf16[32,4096]{1,0:T(8,128)(2,1)} custom-call(bf16[32,32,128]{2,1,0:T(8,128)(2,1)} %all_to_all.16.in_ref), custom_call_target="tpu_custom_call" | custom-call | tf_op jit(solution)/shard_map/pallas_call | solution.py:129
  (5 shorter events, 0.1 us)
Async XLA Ops:
  35.5 3.8 %collective-permute-start = (bf16[32,64,128]{2,1,0:T(8,128)(2,1)S(1)}, bf16[32,64,128]{2,1,0:T(8,128)(2,1)S(1)}, u32[]{:S(2)}, u32[]{:S(2)}) collective-permute-start(bf16[32,64,128]{2,1,0:T(8,128)(2,1)S(1)} %slice.25), channel_id=1, source_target_pairs={{0,1},{1,0},{2,3},{3,2},{4,5},{5,4},{6,7},{7,6},{8,9},{9,8},{10,11... | collective-permute-start | bytes 1572872 | tf_op jit(solution)/shard_map/ppermute | solution.py:109
  40.3 31.2 %all-to-all-start.1 = ((bf16[8,8,2,16,128]{4,3,2,1,0:T(8,128)(2,1)}), bf16[8,8,2,16,128]{4,3,2,1,0:T(8,128)(2,1)S(1)}, u32[]{:S(2)}, u32[]{:S(2)}) async-start(bf16[8,8,2,16,128]{4,3,2,1,0:T(8,128)(2,1)} %broadcast_in_dim.2), calls=%async_computation.1 | async-start | bytes 1048576 | tf_op jit(solution)/shard_map/all_to_all | solution.py:117
  50.2 17.8 %collective-permute-start.1 = (bf16[16,64,128]{2,1,0:T(8,128)(2,1)S(1)}, bf16[16,64,128]{2,1,0:T(8,128)(2,1)S(1)}, u32[]{:S(2)}, u32[]{:S(2)}) collective-permute-start(bf16[16,64,128]{2,1,0:T(8,128)(2,1)S(1)} %slice.26), channel_id=1, source_target_pairs={{0,64},{64,128},{128,192},{192,256},{256,320},{320,384},{384,448},... | collective-permute-start | bytes 786440 | tf_op jit(solution)/shard_map/ppermute | solution.py:108
  68.0 3.4 %collective-permute-start.2 = (bf16[16,64,128]{2,1,0:T(8,128)(2,1)S(1)}, bf16[16,64,128]{2,1,0:T(8,128)(2,1)S(1)}, u32[]{:S(2)}, u32[]{:S(2)}) collective-permute-start(bf16[16,64,128]{2,1,0:T(8,128)(2,1)S(1)} %collective-permute-done.1.back_ref), channel_id=1, source_target_pairs={{0,1},{1,0},{2,3},{3,2},{4,5},{5,4},{6,7},{7,6},{8,9},{9,8},{10,11... | collective-permute-start | bytes 786440 | tf_op jit(solution)/shard_map/ppermute | solution.py:110

commit v2 on v1

--- a/solution.py
+++ b/solution.py
@@ -2,6 +2,7 @@
 
 import jax
 import jax.numpy as jnp
+import numpy as np
 from jax import lax
 from jax.experimental import pallas as pl
 from jax.experimental.pallas import tpu as pltpu
@@ -21,6 +22,7 @@
 BACK = BAND_REACH // SPAN
 TILE = 8
 MASKED = -1e30
+MIB = 2 ** 20
 VMEM = pl.BlockSpec(memory_space=pltpu.VMEM)
 
 
@@ -37,9 +39,11 @@
         out_ref[:, head * HEAD_SIZE:(head + 1) * HEAD_SIZE] = in_ref[head]
 
 
-def attend_kernel(place_ref, own_ref, other_ref, back_ref, back_other_ref, sum_ref, out_ref):
+def attend_kernel(place_ref, own_ref, other_ref, late_ref, late_other_ref, out_ref):
     plane, core = place_ref[0], place_ref[1]
-    near = ((back_ref, own_ref, core), (back_other_ref, other_ref, 1 - core))
+    near = ((late_ref, own_ref, core), (late_other_ref, other_ref, 1 - core))
+    pair = 2 * ROWS
+    sum_from = BACK * pair
     log2e = 1.4426950408889634
     scale = HEAD_SIZE ** -0.5 * log2e
     tile_rows = TILE * ROWS
@@ -55,27 +59,32 @@
     def score(q, k):
         return lax.dot_general(q, k, (((1,), (1,)), ((), ())), preferred_element_type=jnp.float32)
 
+    held = jnp.where(core == 1, late_ref[sum_from:, :], late_other_ref[sum_from:, :])
+    held = held.reshape(-1, 2, SRC * SPAN // BLOCK * SUM, HEAD_SIZE)
+    sums = [held[:, i].reshape(-1, HEAD_SIZE) for i in range(2)]
     for tile in range(SRC // TILE):
         first = tile * TILE
         q = own_ref[first:first + TILE, 2 * ROWS:, :].reshape(tile_rows, HEAD_SIZE)
         qpos = rows_at(first, core * ROWS)
-        reach = jnp.minimum(BAND_REACH, plane * (SRC * SPAN) + qpos + 1)
+        floor = qpos - jnp.minimum(BAND_REACH, plane * (SRC * SPAN) + qpos + 1)
         parts = []
         for behind, here, parity in near:
             for start in range(first - BACK, first + TILE, TILE):
-                source = here if start >= 0 else behind
-                at = start if start >= 0 else start + BACK
-                k = source[at:at + TILE, 0:ROWS, :].reshape(tile_rows, HEAD_SIZE)
-                v = source[at:at + TILE, ROWS:2 * ROWS, :].reshape(tile_rows, HEAD_SIZE)
+                if start >= 0:
+                    both = here[start:start + TILE, :pair, :]
+                else:
+                    both = behind[(start + BACK) * pair:(start + BACK + TILE) * pair, :]
+                    both = both.reshape(TILE, pair, HEAD_SIZE)
+                k = both[:, :ROWS].reshape(tile_rows, HEAD_SIZE)
+                v = both[:, ROWS:].reshape(tile_rows, HEAD_SIZE)
                 s = score(q, k)
-                diff = qpos - cols_at(tile_rows, start, parity * ROWS)
+                kpos = cols_at(tile_rows, start, parity * ROWS)
                 if start == first:
-                    s = jnp.where(diff >= 0, s, MASKED)
+                    s = jnp.where(kpos <= qpos, s, MASKED)
                 elif start < 0 or start == first - BACK:
-                    s = jnp.where(diff < reach, s, MASKED)
+                    s = jnp.where(kpos > floor, s, MASKED)
                 parts.append((s, v))
-        k = sum_ref[:, :, 0].reshape(-1, HEAD_SIZE)
-        v = sum_ref[:, :, 1].reshape(-1, HEAD_SIZE)
+        k, v = sums
         s = score(q, k)
         c = lax.broadcasted_iota(jnp.int32, (1, s.shape[1]), 1)
         spos = (c // SUM) * BLOCK + BLOCK - SUM + c % SUM
@@ -92,6 +101,14 @@
         out_ref[first:first + TILE] = (numer / total).astype(jnp.bfloat16).reshape(TILE, ROWS, HEAD_SIZE)
 
 
+def sum_groups():
+    sizes = [lax.axis_size(axis) for axis in AXES]
+    device = np.arange(np.prod(sizes)).reshape(sizes)
+    along_z = device[..., 1].transpose(1, 2, 0).reshape(-1, sizes[0])
+    along_y = device[..., 0].reshape(-1, sizes[2])
+    return np.concatenate([along_z, along_y]).tolist()
+
+
 def local(queries, keys, values):
     bf16 = jnp.bfloat16
     plane, core = lax.axis_index("z"), lax.axis_index("core")
@@ -100,6 +117,7 @@
         out_shape=jax.ShapeDtypeStruct((HEADS, 3 * ROWS, HEAD_SIZE), bf16),
         in_specs=[VMEM] * 3,
         out_specs=VMEM,
+        compiler_params=pltpu.CompilerParams(vmem_limit_bytes=62 * MIB),
     )(keys, values, queries)
     own = lax.all_to_all(packed, PLANE, 0, 0, tiled=True)
     swap = [(0, 1), (1, 0)]
@@ -107,30 +125,31 @@
     pair = own[:, :2 * ROWS]
     behind = lax.ppermute(pair[SRC - BACK:], "z", [(i, i + 1) for i in range(planes - 1)])
     other = lax.ppermute(pair, "core", swap)
-    behind_other = lax.ppermute(behind, "core", swap)
     step = BLOCK // SPAN
-    picked = [
-        jnp.stack([part[step - 1::step, ROWS - SUM:ROWS], part[step - 1::step, 2 * ROWS - SUM:]], axis=1)
-        for part in (pair, other)
-    ]
-    mine = jnp.where(core == 1, picked[0], picked[1])
-    sums = lax.all_to_all(
-        jnp.broadcast_to(mine[None], (planes, *mine.shape)), "z", 0, 0, tiled=True
-    )
+    mine = jnp.concatenate([
+        own[step - 1::step, ROWS - SUM:ROWS].reshape(-1, HEAD_SIZE),
+        own[step - 1::step, 2 * ROWS - SUM:2 * ROWS].reshape(-1, HEAD_SIZE),
+    ])
+    shares = jnp.broadcast_to(mine[None], (planes, *mine.shape))
+    sums = lax.all_to_all(shares, AXES, 0, 0, axis_index_groups=sum_groups(), tiled=True)
+    late = jnp.concatenate([behind.reshape(-1, HEAD_SIZE), sums.reshape(-1, HEAD_SIZE)])
+    late, other = lax.optimization_barrier((late, other))
+    late_other = lax.ppermute(late, "core", swap)
     place = jnp.stack([plane, core]).astype(jnp.int32)
     out = pl.pallas_call(
         attend_kernel,
         out_shape=jax.ShapeDtypeStruct((SRC, ROWS, HEAD_SIZE), bf16),
-        in_specs=[pl.BlockSpec(memory_space=pltpu.SMEM)] + [VMEM] * 5,
+        in_specs=[pl.BlockSpec(memory_space=pltpu.SMEM)] + [VMEM] * 4,
         out_specs=VMEM,
-        compiler_params=pltpu.CompilerParams(vmem_limit_bytes=48 * 2**20),
-    )(place, own, other, behind, behind_other, sums)
+        compiler_params=pltpu.CompilerParams(vmem_limit_bytes=32 * MIB),
+    )(place, own, other, late, late_other)
     back = lax.all_to_all(out, PLANE, 0, 0, tiled=True)
     return pl.pallas_call(
         unpack_kernel,
         out_shape=jax.ShapeDtypeStruct((ROWS, HEADS * HEAD_SIZE), bf16),
         in_specs=[VMEM],
         out_specs=VMEM,
+        compiler_params=pltpu.CompilerParams(vmem_limit_bytes=8 * MIB),
     )(back)
 
 

time: 95.9 us -> 86 us (0.90)
  the two profiles are of different devices: /device:TPU:72 before, /device:TPU:8 now
where the time goes in v2:
time: 86 us; the launch traced here: 85.6 us
  blocking collectives  52 us (60%)
  starting transfers between devices  18.2 us (21%)
  Pallas kernels  7.86 us (9%)
  waiting for transfers between devices  6.45 us (8%)
  local copies, waits for them, and re-layouts  0.94 us (1%)
    all_to_all x1, blocking collectives, local(): own = lax.all_to_all(packed, PLANE, 0, 0, tiled=True)  33.3 us
    all_to_all x1, blocking collectives, local(): back = lax.all_to_all(out, PLANE, 0, 0, tiled=True)  18.6 us
    ppermute x1, starting transfers between devices, local(): late_other = lax.ppermute(late, 'core', swap)  5.3 us
    pallas_call x1, Pallas kernels, local(): pl.pallas_call(attend_kernel, out_shape=jax.ShapeDtypeStruct((SRC, ROWS,...  4.97 us
    ppermute x1, starting transfers between devices, local(): other = lax.ppermute(pair, 'core', swap)  4.76 us
    ppermute x1, waiting for transfers between devices, local(): lax.ppermute(pair[SRC - BACK:], 'z', [(i, i + 1) for i in range(planes -...  4.64 us
    ppermute x1, starting transfers between devices, local(): lax.ppermute(pair[SRC - BACK:], 'z', [(i, i + 1) for i in range(planes -...  4.29 us
    all_to_all x1, starting transfers between devices, local(): lax.all_to_all(shares, AXES, 0, 0, axis_index_groups=sum_groups(), tiled=...  3.86 us
  transfers between devices with their start and end apart: 4, of which 2 were waited for; matrix products, arithmetic and copies ran while one was open for 0% of the time, Pallas kernels for 0%

profile of v2, /device:TPU:8, one launch (start us, length us, event | category | flops | bytes accessed | tf_op | source)
XLA Modules:
  0.0 85.6 jit_solution(6946913223565165484)
XLA Ops:
  0.0 2.1 %shard_map.37 = bf16[32,96,128]{2,1,0:T(8,128)(2,1)} custom-call(bf16[32,4096]{1,0:T(8,128)(2,1)} %k_ref.1, bf16[32,4096]{1,0:T(8,128)(2,1)} %v_ref.1, bf16[32,4096]{1,0:T(8,128)(2,1)} %q_ref.1), custom_call_target="tpu_custom_call" | custom-call | tf_op jit(solution)/shard_map/pallas_call | solution.py:115
  2.1 33.3 %all_to_all.15.own_ref = bf16[32,96,128]{2,1,0:T(8,128)(2,1)S(1)} all-to-all(bf16[32,96,128]{2,1,0:T(8,128)(2,1)} %shard_map.37), channel_id=1, replica_groups=mesh['z'=8,'x'=4,'y'=8,'core'=2] {'x','y'}, dimensions={0} | all-to-all | bytes 1572864 | tf_op jit(solution)/shard_map/all_to_all | solution.py:122
  35.5 0.9 broadcast_in_dim.2
  36.3 3.9 %all-to-all-start.1 = ((bf16[8,256,128]{2,1,0:T(8,128)(2,1)}), bf16[8,256,128]{2,1,0:T(8,128)(2,1)S(1)}, u32[]{:S(2)}, u32[]{:S(2)}) async-start(bf16[8,256,128]{2,1,0:T(8,128)(2,1)} %broadcast_in_dim.2), calls=%async_computation.1 | async-start | bytes 1048576 | tf_op jit(solution)/shard_map/all_to_all | solution.py:134
  40.2 4.3 %collective-permute-start = (bf16[16,64,128]{2,1,0:T(8,128)(2,1)S(1)}, bf16[16,64,128]{2,1,0:T(8,128)(2,1)S(1)}, u32[]{:S(2)}, u32[]{:S(2)}) collective-permute-start(bf16[16,64,128]{2,1,0:T(8,128)(2,1)S(1)} %slice.17), channel_id=1, source_target_pairs={{0,64},{64,128},{128,192},{192,256},{256,320},{320,384},{384,448},... | collective-permute-start | bytes 786440 | tf_op jit(solution)/shard_map/ppermute | solution.py:126
  44.5 0.1 slice.18
  44.6 4.8 %collective-permute-start.1 = (bf16[32,64,128]{2,1,0:T(8,128)(2,1)S(1)}, bf16[32,64,128]{2,1,0:T(8,128)(2,1)S(1)}, u32[]{:S(2)}, u32[]{:S(2)}) collective-permute-start(bf16[32,64,128]{2,1,0:T(8,128)(2,1)S(1)} %slice.18), channel_id=1, source_target_pairs={{0,1},{1,0},{2,3},{3,2},{4,5},{5,4},{6,7},{7,6},{8,9},{9,8},{10,11... | collective-permute-start | bytes 1572872 | tf_op jit(solution)/shard_map/ppermute | solution.py:127
  49.4 4.6 %collective-permute-done = bf16[16,64,128]{2,1,0:T(8,128)(2,1)S(1)} collective-permute-done((bf16[16,64,128]{2,1,0:T(8,128)(2,1)S(1)}, bf16[16,64,128]{2,1,0:T(8,128)(2,1)S(1)}, u32[]{:S(2)}, u32[]{:S(2)}) %collective-permute-start) | collective-permute-done | bytes 262176 | tf_op jit(solution)/shard_map/ppermute | solution.py:126
  54.0 0.0 all-to-all-done.1
  54.0 0.1 pad_maximum_fusion.late_ref
  54.1 0.0 collective-permute-done.1.other_ref
  54.1 5.3 %collective-permute-start.2 = (bf16[3072,128]{1,0:T(8,128)(2,1)S(1)}, bf16[3072,128]{1,0:T(8,128)(2,1)S(1)}, u32[]{:S(2)}, u32[]{:S(2)}) collective-permute-start(bf16[3072,128]{1,0:T(8,128)(2,1)S(1)} %pad_maximum_fusion.late_ref), channel_id=1, source_target_pairs={{0,1},{1,0},{2,3},{3,2},{4,5},{5,4},{6,7},{7,6},{8,9},{9,8},{10,11... | collective-permute-start | bytes 2359304 | tf_op jit(solution)/shard_map/ppermute | solution.py:137
  59.4 0.1 pad_add_fusion.place_ref
  59.5 1.8 %collective-permute-done.2.late_other_ref = bf16[3072,128]{1,0:T(8,128)(2,1)S(1)} collective-permute-done((bf16[3072,128]{1,0:T(8,128)(2,1)S(1)}, bf16[3072,128]{1,0:T(8,128)(2,1)S(1)}, u32[]{:S(2)}, u32[]{:S(2)}) %collective-permute-start.2) | collective-permute-done | bytes 786464 | tf_op jit(solution)/shard_map/ppermute | solution.py:137
  61.3 5.0 %shard_map.38 = bf16[32,32,128]{2,1,0:T(8,128)(2,1)S(1)} custom-call(s32[2]{0:T(128)S(1)} %pad_add_fusion.place_ref, bf16[32,96,128]{2,1,0:T(8,128)(2,1)S(1)} %all_to_all.15.own_ref, bf16[32,64,128]{2,1,0:T(8,128)(2,1)S(1)} %collective-permute-done.1.other_ref, bf16[3072,128]{1,0:T(8,128)(2,1)S(1)} %pad_maximum_fusion.late_ref, ...), custom_call_target="tpu_custom_call" | custom-call | tf_op jit(solution)/shard_map/pallas_call | solution.py:139
  66.2 18.6 %all_to_all.16.in_ref = bf16[32,32,128]{2,1,0:T(8,128)(2,1)S(1)} all-to-all(bf16[32,32,128]{2,1,0:T(8,128)(2,1)S(1)} %shard_map.38), channel_id=1, replica_groups=mesh['z'=8,'x'=4,'y'=8,'core'=2] {'x','y'}, dimensions={0} | all-to-all | bytes 524288 | tf_op jit(solution)/shard_map/all_to_all | solution.py:146
  84.9 0.7 shard_map.39
  (3 shorter events, 0.0 us)
Async XLA Ops:
  36.3 17.7 %all-to-all-start.1 = ((bf16[8,256,128]{2,1,0:T(8,128)(2,1)}), bf16[8,256,128]{2,1,0:T(8,128)(2,1)S(1)}, u32[]{:S(2)}, u32[]{:S(2)}) async-start(bf16[8,256,128]{2,1,0:T(8,128)(2,1)} %broadcast_in_dim.2), calls=%async_computation.1 | async-start | bytes 1048576 | tf_op jit(solution)/shard_map/all_to_all | solution.py:134
  40.2 13.8 %collective-permute-start = (bf16[16,64,128]{2,1,0:T(8,128)(2,1)S(1)}, bf16[16,64,128]{2,1,0:T(8,128)(2,1)S(1)}, u32[]{:S(2)}, u32[]{:S(2)}) collective-permute-start(bf16[16,64,128]{2,1,0:T(8,128)(2,1)S(1)} %slice.17), channel_id=1, source_target_pairs={{0,64},{64,128},{128,192},{192,256},{256,320},{320,384},{384,448},... | collective-permute-start | bytes 786440 | tf_op jit(solution)/shard_map/ppermute | solution.py:126
  44.6 9.5 %collective-permute-start.1 = (bf16[32,64,128]{2,1,0:T(8,128)(2,1)S(1)}, bf16[32,64,128]{2,1,0:T(8,128)(2,1)S(1)}, u32[]{:S(2)}, u32[]{:S(2)}) collective-permute-start(bf16[32,64,128]{2,1,0:T(8,128)(2,1)S(1)} %slice.18), channel_id=1, source_target_pairs={{0,1},{1,0},{2,3},{3,2},{4,5},{5,4},{6,7},{7,6},{8,9},{9,8},{10,11... | collective-permute-start | bytes 1572872 | tf_op jit(solution)/shard_map/ppermute | solution.py:127
  54.1 7.2 %collective-permute-start.2 = (bf16[3072,128]{1,0:T(8,128)(2,1)S(1)}, bf16[3072,128]{1,0:T(8,128)(2,1)S(1)}, u32[]{:S(2)}, u32[]{:S(2)}) collective-permute-start(bf16[3072,128]{1,0:T(8,128)(2,1)S(1)} %pad_maximum_fusion.late_ref), channel_id=1, source_target_pairs={{0,1},{1,0},{2,3},{3,2},{4,5},{5,4},{6,7},{7,6},{8,9},{9,8},{10,11... | collective-permute-start | bytes 2359304 | tf_op jit(solution)/shard_map/ppermute | solution.py:137

commit v3 on v2

v3 whole, which is shorter than its diff:
```python
import functools

import jax
import jax.numpy as jnp
import numpy as np
from jax import lax
from jax.experimental import pallas as pl
from jax.experimental.pallas import tpu as pltpu
from jax.sharding import Mesh
from jax.sharding import PartitionSpec as P

HEAD_SIZE = 128
BLOCK = 256
SUM = 16
BAND_REACH = 1024
AXES = ("z", "x", "y", "core")
PLANE = ("x", "y")
ROWS = 32
HEADS = 32
SPAN = 2 * ROWS
SRC = 32
BACK = BAND_REACH // SPAN
TILE = 8
MASKED = -1e30
SCALE = HEAD_SIZE ** -0.5 * 1.4426950408889634
MIB = 2 ** 20
VMEM = pl.BlockSpec(memory_space=pltpu.VMEM)


def pack_kernel(k_ref, v_ref, q_ref, out_ref, held, slabs, in_sems, out_sems):
    half = HEADS // 2
    loads, stores = [], []
    for i in range(2):
        cols = pl.ds(i * half * HEAD_SIZE, half * HEAD_SIZE)
        for j, ref in enumerate((k_ref, v_ref, q_ref)):
            loads.append(pltpu.make_async_copy(ref.at[:, cols], held.at[j, :, cols], in_sems.at[i, j]))
        heads = pl.ds(i * half, half)
        stores.append(pltpu.make_async_copy(slabs.at[heads], out_ref.at[heads], out_sems.at[i]))
    for load in loads:
        load.start()
    for i in range(2):
        for j in range(3):
            loads[3 * i + j].wait()
            for head in range(i * half, (i + 1) * half):
                cols = slice(head * HEAD_SIZE, (head + 1) * HEAD_SIZE)
                slabs[head, j * ROWS:(j + 1) * ROWS, :] = held[j, :, cols]
        stores[i].start()
    for store in stores:
        store.wait()


def unpack_kernel(in_ref, out_ref):
    for head in range(HEADS):
        out_ref[:, head * HEAD_SIZE:(head + 1) * HEAD_SIZE] = in_ref[head]


def row_positions(start, offset):
    r = lax.broadcasted_iota(jnp.int32, (TILE * ROWS, 1), 0)
    return (r // ROWS) * SPAN + r % ROWS + start * SPAN + offset


def col_positions(start, offset):
    c = lax.broadcasted_iota(jnp.int32, (1, TILE * ROWS), 1)
    return (c // ROWS) * SPAN + c % ROWS + start * SPAN + offset


def score(q, k):
    return lax.dot_general(q, k, (((1,), (1,)), ((), ())), preferred_element_type=jnp.float32)


def weigh(parts, top):
    total = numer = 0.0
    for s, v in parts:
        weight = jnp.exp2((s - top) * SCALE)
        total = total + jnp.sum(weight, axis=1, keepdims=True)
        numer = numer + jnp.dot(weight.astype(jnp.bfloat16), v, preferred_element_type=jnp.float32)
    return total, numer


def here_kernel(place_ref, own_ref, other_ref, numer_ref, top_ref, total_ref):
    core = place_ref[1]
    rows = TILE * ROWS
    for tile in range(SRC // TILE):
        first = tile * TILE
        q = own_ref[first:first + TILE, 2 * ROWS:, :].reshape(rows, HEAD_SIZE)
        qpos = row_positions(first, core * ROWS)
        parts = []
        for here, parity in ((own_ref, core), (other_ref, 1 - core)):
            for start in range(max(0, first - BACK), first + TILE, TILE):
                k = here[start:start + TILE, 0:ROWS, :].reshape(rows, HEAD_SIZE)
                v = here[start:start + TILE, ROWS:2 * ROWS, :].reshape(rows, HEAD_SIZE)
                s = score(q, k)
                kpos = col_positions(start, parity * ROWS)
                if start == first:
                    s = jnp.where(kpos <= qpos, s, MASKED)
                elif start == first - BACK:
                    s = jnp.where(kpos > qpos - BAND_REACH, s, MASKED)
                parts.append((s, v))
        top = functools.reduce(jnp.maximum, [jnp.max(s, axis=1, keepdims=True) for s, _ in parts])
        total, numer = weigh(parts, top)
        at = slice(tile * rows, (tile + 1) * rows)
        numer_ref[at] = numer
        top_ref[at] = jnp.broadcast_to(top, (rows, HEAD_SIZE))
        total_ref[at] = jnp.broadcast_to(total, (rows, HEAD_SIZE))


def late_kernel(planes, place_ref, own_ref, late_ref, late_other_ref, numer_ref, top_ref, total_ref, out_ref):
    plane, core = place_ref[0], place_ref[1]
    rows, pair = TILE * ROWS, 2 * ROWS
    sum_from = BACK * pair
    per_plane = SRC * SPAN // BLOCK * SUM

    def attend(k_sum, v_sum):
        c = lax.broadcasted_iota(jnp.int32, (1, k_sum.shape[0]), 1)
        spos = (c // SUM) * BLOCK + BLOCK - SUM + c % SUM
        for tile in range(SRC // TILE):
            first = tile * TILE
            at = slice(tile * rows, (tile + 1) * rows)
            q = own_ref[first:first + TILE, 2 * ROWS:, :].reshape(rows, HEAD_SIZE)
            qpos = row_positions(first, core * ROWS)
            floor = qpos - jnp.minimum(BAND_REACH, plane * (SRC * SPAN) + qpos + 1)
            parts = []
            for behind, parity in ((late_ref, core), (late_other_ref, 1 - core)):
                for start in range(first - BACK, 0, TILE):
                    both = behind[(start + BACK) * pair:(start + BACK + TILE) * pair, :]
                    both = both.reshape(TILE, pair, HEAD_SIZE)
                    s = score(q, both[:, :ROWS].reshape(rows, HEAD_SIZE))
                    s = jnp.where(col_positions(start, parity * ROWS) > floor, s, MASKED)
                    parts.append((s, both[:, ROWS:].reshape(rows, HEAD_SIZE)))
            far = plane * (SRC * SPAN) + qpos - BAND_REACH
            parts.append((jnp.where(spos <= far, score(q, k_sum), MASKED), v_sum))
            near_top = top_ref[at]
            tops = [jnp.max(s, axis=1, keepdims=True) for s, _ in parts]
            top = functools.reduce(jnp.maximum, tops, near_top)
            total, numer = weigh(parts, top[:, :1])
            keep = jnp.exp2((near_top - top) * SCALE)
            numer = numer + keep * numer_ref[at]
            total = total + keep * total_ref[at]
            out_ref[first:first + TILE] = (numer / total).astype(jnp.bfloat16).reshape(TILE, ROWS, HEAD_SIZE)

    for level in range(2, planes + 1, 2):

        @pl.when((plane >= level - 2) & (plane < level))
        def _(level=level):
            held = slice(sum_from, sum_from + level * 2 * per_plane)
            held = jnp.where(core == 1, late_ref[held, :], late_other_ref[held, :])
            held = held.reshape(level, 2, per_plane, HEAD_SIZE)
            attend(held[:, 0].reshape(-1, HEAD_SIZE), held[:, 1].reshape(-1, HEAD_SIZE))


def sum_groups():
    sizes = [lax.axis_size(axis) for axis in AXES]
    device = np.arange(np.prod(sizes)).reshape(sizes)
    along_z = device[..., 1].transpose(1, 2, 0).reshape(-1, sizes[0])
    along_y = device[..., 0].reshape(-1, sizes[2])
    return np.concatenate([along_z, along_y]).tolist()


def local(queries, keys, values):
    bf16 = jnp.bfloat16
    plane, core = lax.axis_index("z"), lax.axis_index("core")
    packed = pl.pallas_call(
        pack_kernel,
        out_shape=jax.ShapeDtypeStruct((HEADS, 3 * ROWS, HEAD_SIZE), bf16),
        in_specs=[pl.BlockSpec(memory_space=pltpu.HBM)] * 3,
        out_specs=pl.BlockSpec(memory_space=pltpu.HBM),
        scratch_shapes=[
            pltpu.VMEM((3, ROWS, HEADS * HEAD_SIZE), bf16),
            pltpu.VMEM((HEADS, 3 * ROWS, HEAD_SIZE), bf16),
            pltpu.SemaphoreType.DMA((2, 3)),
            pltpu.SemaphoreType.DMA((2,)),
        ],
        compiler_params=pltpu.CompilerParams(vmem_limit_bytes=62 * MIB),
    )(keys, values, queries)
    own = lax.all_to_all(packed, PLANE, 0, 0, tiled=True)
    swap = [(0, 1), (1, 0)]
    planes = lax.axis_size("z")
    pair = own[:, :2 * ROWS]
    behind = lax.ppermute(pair[SRC - BACK:], "z", [(i, i + 1) for i in range(planes - 1)])
    other = lax.ppermute(pair, "core", swap)
    step = BLOCK // SPAN
    mine = jnp.concatenate([
        own[step - 1::step, ROWS - SUM:ROWS].reshape(-1, HEAD_SIZE),
        own[step - 1::step, 2 * ROWS - SUM:2 * ROWS].reshape(-1, HEAD_SIZE),
    ])
    shares = jnp.broadcast_to(mine[None], (planes, *mine.shape))
    sums = lax.all_to_all(shares, AXES, 0, 0, axis_index_groups=sum_groups(), tiled=True)
    late = jnp.concatenate([behind.reshape(-1, HEAD_SIZE), sums.reshape(-1, HEAD_SIZE)])
    late, other = lax.optimization_barrier((late, other))
    late_other = lax.ppermute(late, "core", swap)
    place = jnp.stack([plane, core]).astype(jnp.int32)
    smem = pl.BlockSpec(memory_space=pltpu.SMEM)
    part = jax.ShapeDtypeStruct((SRC * ROWS, HEAD_SIZE), jnp.float32)
    near = pl.pallas_call(
        here_kernel,
        out_shape=(part, part, part),
        in_specs=[smem] + [VMEM] * 2,
        out_specs=(VMEM,) * 3,
        compiler_params=pltpu.CompilerParams(vmem_limit_bytes=16 * MIB),
        cost_estimate=pl.CostEstimate(flops=4 * 10 ** 8, transcendentals=10 ** 6, bytes_accessed=3 * 10 ** 6),
    )(place, own, other)
    out = pl.pallas_call(
        functools.partial(late_kernel, planes),
        out_shape=jax.ShapeDtypeStruct((SRC, ROWS, HEAD_SIZE), bf16),
        in_specs=[smem] + [VMEM] * 6,
        out_specs=VMEM,
        compiler_params=pltpu.CompilerParams(vmem_limit_bytes=16 * MIB),
    )(place, own, late, late_other, *near)
    back = lax.all_to_all(out, PLANE, 0, 0, tiled=True)
    return pl.pallas_call(
        unpack_kernel,
        out_shape=jax.ShapeDtypeStruct((ROWS, HEADS * HEAD_SIZE), bf16),
        in_specs=[VMEM],
        out_specs=VMEM,
        compiler_params=pltpu.CompilerParams(vmem_limit_bytes=8 * MIB),
    )(back)


def solution(mesh):
    chips = Mesh(mesh.devices.reshape(8, 4, 8, 2), AXES)
    placed = P(AXES, None)
    return jax.shard_map(
        local, mesh=chips, in_specs=(placed,) * 3, out_specs=placed, check_vma=False
    )
```

time: 86 us -> 84.4 us (0.981)
  waiting for transfers between devices: 6.45 us -> 4.65 us
    ppermute x1, waiting for transfers between devices: 1.81 us -> 0.01 us  [local(): late_other = lax.ppermute(late, 'core', swap)]
    pallas_call x1 -> x2, Pallas kernels: 4.97 us -> 5.58 us  [the longest x1 2.83 us: local(): pl.pallas_call(functools.partial(late_kernel, planes), out_shape=jax.Shap...]
  transfers between devices with their start and end apart: 4 -> 4, of which waited for: 2 -> 1; matrix products, arithmetic and copies ran while one was open for 0% -> 0% of each run, Pallas kernels for 0% -> 3%
where the time goes in v3:
time: 84.4 us; the launch traced here: 84 us
  blocking collectives  51.6 us (61%)
  starting transfers between devices  18.2 us (22%)
  Pallas kernels  8.37 us (10%)
  waiting for transfers between devices  4.65 us (6%)
  local copies, waits for them, and re-layouts  0.94 us (1%)
    all_to_all x1, blocking collectives, local(): own = lax.all_to_all(packed, PLANE, 0, 0, tiled=True)  33.3 us
    all_to_all x1, blocking collectives, local(): back = lax.all_to_all(out, PLANE, 0, 0, tiled=True)  18.3 us
    ppermute x1, starting transfers between devices, local(): late_other = lax.ppermute(late, 'core', swap)  5.3 us
    ppermute x1, starting transfers between devices, local(): other = lax.ppermute(pair, 'core', swap)  4.76 us
    ppermute x1, waiting for transfers between devices, local(): lax.ppermute(pair[SRC - BACK:], 'z', [(i, i + 1) for i in range(planes -...  4.64 us
    ppermute x1, starting transfers between devices, local(): lax.ppermute(pair[SRC - BACK:], 'z', [(i, i + 1) for i in range(planes -...  4.29 us
    all_to_all x1, starting transfers between devices, local(): lax.all_to_all(shares, AXES, 0, 0, axis_index_groups=sum_groups(), tiled=...  3.86 us
    pallas_call x1, Pallas kernels, local(): pl.pallas_call(functools.partial(late_kernel, planes), out_shape=jax.Shap...  2.83 us
  transfers between devices with their start and end apart: 4, of which 1 were waited for; matrix products, arithmetic and copies ran while one was open for 0% of the time, Pallas kernels for 3%

profile of v3, /device:TPU:8, one launch (start us, length us, event | category | flops | bytes accessed | tf_op | source)
XLA Modules:
  0.0 84.0 jit_solution(13823031735028189064)
XLA Ops:
  0.0 2.1 %shard_map.37 = bf16[32,96,128]{2,1,0:T(8,128)(2,1)} custom-call(bf16[32,4096]{1,0:T(8,128)(2,1)} %k_ref.1, bf16[32,4096]{1,0:T(8,128)(2,1)} %v_ref.1, bf16[32,4096]{1,0:T(8,128)(2,1)} %q_ref.1), custom_call_target="tpu_custom_call" | custom-call | tf_op jit(solution)/shard_map/pallas_call | solution.py:162
  2.1 33.3 %all_to_all.15.own_ref = bf16[32,96,128]{2,1,0:T(8,128)(2,1)S(1)} all-to-all(bf16[32,96,128]{2,1,0:T(8,128)(2,1)} %shard_map.37), channel_id=1, replica_groups=mesh['z'=8,'x'=4,'y'=8,'core'=2] {'x','y'}, dimensions={0} | all-to-all | bytes 1572864 | tf_op jit(solution)/shard_map/all_to_all | solution.py:175
  35.4 0.9 %broadcast_in_dim.2 = bf16[8,256,128]{2,1,0:T(8,128)(2,1)} broadcast(bf16[256,128]{1,0:T(8,128)(2,1)S(1)} %pad_maximum_fusion.1), dimensions={1,2} | broadcast | bytes 589824 | tf_op jit(solution)/shard_map/broadcast_in_dim | solution.py:186
  36.3 3.9 %all-to-all-start.1 = ((bf16[8,256,128]{2,1,0:T(8,128)(2,1)}), bf16[8,256,128]{2,1,0:T(8,128)(2,1)S(1)}, u32[]{:S(2)}, u32[]{:S(2)}) async-start(bf16[8,256,128]{2,1,0:T(8,128)(2,1)} %broadcast_in_dim.2), calls=%async_computation.1 | async-start | bytes 1048576 | tf_op jit(solution)/shard_map/all_to_all | solution.py:187
  40.2 4.3 %collective-permute-start = (bf16[16,64,128]{2,1,0:T(8,128)(2,1)S(1)}, bf16[16,64,128]{2,1,0:T(8,128)(2,1)S(1)}, u32[]{:S(2)}, u32[]{:S(2)}) collective-permute-start(bf16[16,64,128]{2,1,0:T(8,128)(2,1)S(1)} %slice.17), channel_id=1, source_target_pairs={{0,64},{64,128},{128,192},{192,256},{256,320},{320,384},{384,448},... | collective-permute-start | bytes 786440 | tf_op jit(solution)/shard_map/ppermute | solution.py:179
  44.5 0.1 slice.18
  44.5 4.8 %collective-permute-start.1 = (bf16[32,64,128]{2,1,0:T(8,128)(2,1)S(1)}, bf16[32,64,128]{2,1,0:T(8,128)(2,1)S(1)}, u32[]{:S(2)}, u32[]{:S(2)}) collective-permute-start(bf16[32,64,128]{2,1,0:T(8,128)(2,1)S(1)} %slice.18), channel_id=1, source_target_pairs={{0,1},{1,0},{2,3},{3,2},{4,5},{5,4},{6,7},{7,6},{8,9},{9,8},{10,11... | collective-permute-start | bytes 1572872 | tf_op jit(solution)/shard_map/ppermute | solution.py:180
  49.3 4.6 %collective-permute-done = bf16[16,64,128]{2,1,0:T(8,128)(2,1)S(1)} collective-permute-done((bf16[16,64,128]{2,1,0:T(8,128)(2,1)S(1)}, bf16[16,64,128]{2,1,0:T(8,128)(2,1)S(1)}, u32[]{:S(2)}, u32[]{:S(2)}) %collective-permute-start) | collective-permute-done | bytes 262176 | tf_op jit(solution)/shard_map/ppermute | solution.py:179
  53.9 0.0 all-to-all-done.1
  53.9 0.1 pad_maximum_fusion.late_ref
  54.0 0.0 collective-permute-done.1.other_ref
  54.0 5.3 %collective-permute-start.2 = (bf16[3072,128]{1,0:T(8,128)(2,1)S(1)}, bf16[3072,128]{1,0:T(8,128)(2,1)S(1)}, u32[]{:S(2)}, u32[]{:S(2)}) collective-permute-start(bf16[3072,128]{1,0:T(8,128)(2,1)S(1)} %pad_maximum_fusion.late_ref), channel_id=1, source_target_pairs={{0,1},{1,0},{2,3},{3,2},{4,5},{5,4},{6,7},{7,6},{8,9},{9,8},{10,11... | collective-permute-start | bytes 2359304 | tf_op jit(solution)/shard_map/ppermute | solution.py:190
  59.3 0.1 pad_add_fusion.place_ref
  59.4 2.7 %shard_map.38 = (f32[1024,128]{1,0:T(8,128)S(1)}, f32[1024,128]{1,0:T(8,128)S(1)}, f32[1024,128]{1,0:T(8,128)S(1)}) custom-call(s32[2]{0:T(128)S(1)} %pad_add_fusion.place_ref, bf16[32,96,128]{2,1,0:T(8,128)(2,1)S(1)} %all_to_all.15.own_ref, bf16[32,64,128]{2,1,0:T(8,128)(2,1)S(1)} %collective-permute-done.1.other_ref), custom_call_target="tpu_custom_call" | custom-call | flops 400000000 | bytes 3000000 | tf_op jit(solution)/shard_map/pallas_call | solution.py:194
  62.2 0.0 collective-permute-done.2.late_other_ref
  62.2 2.8 %shard_map.39 = bf16[32,32,128]{2,1,0:T(8,128)(2,1)S(1)} custom-call(s32[2]{0:T(128)S(1)} %pad_add_fusion.place_ref, bf16[32,96,128]{2,1,0:T(8,128)(2,1)S(1)} %all_to_all.15.own_ref, bf16[3072,128]{1,0:T(8,128)(2,1)S(1)} %pad_maximum_fusion.late_ref, bf16[3072,128]{1,0:T(8,128)(2,1)S(1)} %collective-permute-done.2.late_other_ref, ...), custom_call_target="tpu_custom_call" | custom-call | tf_op jit(solution)/shard_map/pallas_call | solution.py:202
  65.0 18.3 %all_to_all.16.in_ref = bf16[32,32,128]{2,1,0:T(8,128)(2,1)S(1)} all-to-all(bf16[32,32,128]{2,1,0:T(8,128)(2,1)S(1)} %shard_map.39), channel_id=1, replica_groups=mesh['z'=8,'x'=4,'y'=8,'core'=2] {'x','y'}, dimensions={0} | all-to-all | bytes 524288 | tf_op jit(solution)/shard_map/all_to_all | solution.py:209
  83.3 0.7 shard_map.40
  (3 shorter events, 0.0 us)
Async XLA Ops:
  36.3 17.7 %all-to-all-start.1 = ((bf16[8,256,128]{2,1,0:T(8,128)(2,1)}), bf16[8,256,128]{2,1,0:T(8,128)(2,1)S(1)}, u32[]{:S(2)}, u32[]{:S(2)}) async-start(bf16[8,256,128]{2,1,0:T(8,128)(2,1)} %broadcast_in_dim.2), calls=%async_computation.1 | async-start | bytes 1048576 | tf_op jit(solution)/shard_map/all_to_all | solution.py:187
  40.2 13.8 %collective-permute-start = (bf16[16,64,128]{2,1,0:T(8,128)(2,1)S(1)}, bf16[16,64,128]{2,1,0:T(8,128)(2,1)S(1)}, u32[]{:S(2)}, u32[]{:S(2)}) collective-permute-start(bf16[16,64,128]{2,1,0:T(8,128)(2,1)S(1)} %slice.17), channel_id=1, source_target_pairs={{0,64},{64,128},{128,192},{192,256},{256,320},{320,384},{384,448},... | collective-permute-start | bytes 786440 | tf_op jit(solution)/shard_map/ppermute | solution.py:179
  44.5 9.5 %collective-permute-start.1 = (bf16[32,64,128]{2,1,0:T(8,128)(2,1)S(1)}, bf16[32,64,128]{2,1,0:T(8,128)(2,1)S(1)}, u32[]{:S(2)}, u32[]{:S(2)}) collective-permute-start(bf16[32,64,128]{2,1,0:T(8,128)(2,1)S(1)} %slice.18), channel_id=1, source_target_pairs={{0,1},{1,0},{2,3},{3,2},{4,5},{5,4},{6,7},{7,6},{8,9},{9,8},{10,11... | collective-permute-start | bytes 1572872 | tf_op jit(solution)/shard_map/ppermute | solution.py:180
  54.0 8.1 %collective-permute-start.2 = (bf16[3072,128]{1,0:T(8,128)(2,1)S(1)}, bf16[3072,128]{1,0:T(8,128)(2,1)S(1)}, u32[]{:S(2)}, u32[]{:S(2)}) collective-permute-start(bf16[3072,128]{1,0:T(8,128)(2,1)S(1)} %pad_maximum_fusion.late_ref), channel_id=1, source_target_pairs={{0,1},{1,0},{2,3},{3,2},{4,5},{5,4},{6,7},{7,6},{8,9},{9,8},{10,11... | collective-permute-start | bytes 2359304 | tf_op jit(solution)/shard_map/ppermute | solution.py:190

commit v4 on v3

--- a/solution.py
+++ b/solution.py
@@ -110,7 +110,7 @@
     sum_from = BACK * pair
     per_plane = SRC * SPAN // BLOCK * SUM
 
-    def attend(k_sum, v_sum):
+    def attend(k_sum, v_sum, first_plane):
         c = lax.broadcasted_iota(jnp.int32, (1, k_sum.shape[0]), 1)
         spos = (c // SUM) * BLOCK + BLOCK - SUM + c % SUM
         for tile in range(SRC // TILE):
@@ -121,7 +121,7 @@
             floor = qpos - jnp.minimum(BAND_REACH, plane * (SRC * SPAN) + qpos + 1)
             parts = []
             for behind, parity in ((late_ref, core), (late_other_ref, 1 - core)):
-                for start in range(first - BACK, 0, TILE):
+                for start in () if first_plane else range(first - BACK, 0, TILE):
                     both = behind[(start + BACK) * pair:(start + BACK + TILE) * pair, :]
                     both = both.reshape(TILE, pair, HEAD_SIZE)
                     s = score(q, both[:, :ROWS].reshape(rows, HEAD_SIZE))
@@ -138,14 +138,14 @@
             total = total + keep * total_ref[at]
             out_ref[first:first + TILE] = (numer / total).astype(jnp.bfloat16).reshape(TILE, ROWS, HEAD_SIZE)
 
-    for level in range(2, planes + 1, 2):
-
-        @pl.when((plane >= level - 2) & (plane < level))
+    for level in range(1, planes + 1):
+
+        @pl.when(plane == level - 1)
         def _(level=level):
             held = slice(sum_from, sum_from + level * 2 * per_plane)
             held = jnp.where(core == 1, late_ref[held, :], late_other_ref[held, :])
             held = held.reshape(level, 2, per_plane, HEAD_SIZE)
-            attend(held[:, 0].reshape(-1, HEAD_SIZE), held[:, 1].reshape(-1, HEAD_SIZE))
+            attend(held[:, 0].reshape(-1, HEAD_SIZE), held[:, 1].reshape(-1, HEAD_SIZE), level == 1)
 
 
 def sum_groups():

time: 84.4 us -> 83.9 us (level)
  the two profiles are of different devices: /device:TPU:8 before, /device:TPU:72 now
where the time goes in v4:
time: 83.9 us; the launch traced here: 83.5 us
  blocking collectives  52.8 us (63%)
  starting transfers between devices  15.5 us (18%)
  Pallas kernels  8.4 us (10%)
  waiting for transfers between devices  5.68 us (7%)
  local copies, waits for them, and re-layouts  0.94 us (1%)
    all_to_all x1, blocking collectives, local(): own = lax.all_to_all(packed, PLANE, 0, 0, tiled=True)  33.3 us
    all_to_all x1, blocking collectives, local(): back = lax.all_to_all(out, PLANE, 0, 0, tiled=True)  19.4 us
    ppermute x1, waiting for transfers between devices, local(): lax.ppermute(pair[SRC - BACK:], 'z', [(i, i + 1) for i in range(planes -...  5.67 us
    ppermute x1, starting transfers between devices, local(): lax.ppermute(pair[SRC - BACK:], 'z', [(i, i + 1) for i in range(planes -...  4.28 us
    all_to_all x1, starting transfers between devices, local(): lax.all_to_all(shares, AXES, 0, 0, axis_index_groups=sum_groups(), tiled=...  3.86 us
    ppermute x1, starting transfers between devices, local(): other = lax.ppermute(pair, 'core', swap)  3.85 us
    ppermute x1, starting transfers between devices, local(): late_other = lax.ppermute(late, 'core', swap)  3.53 us
    pallas_call x1, Pallas kernels, local(): pl.pallas_call(functools.partial(late_kernel, planes), out_shape=jax.Shap...  2.85 us
  transfers between devices with their start and end apart: 4, of which 1 were waited for; matrix products, arithmetic and copies ran while one was open for 0% of the time, Pallas kernels for 3%

profile of v4, /device:TPU:72, one launch (start us, length us, event | category | flops | bytes accessed | tf_op | source)
XLA Modules:
  0.0 83.5 jit_solution(9723265004595475568)
XLA Ops:
  0.0 2.1 %shard_map.37 = bf16[32,96,128]{2,1,0:T(8,128)(2,1)} custom-call(bf16[32,4096]{1,0:T(8,128)(2,1)} %k_ref.1, bf16[32,4096]{1,0:T(8,128)(2,1)} %v_ref.1, bf16[32,4096]{1,0:T(8,128)(2,1)} %q_ref.1), custom_call_target="tpu_custom_call" | custom-call | tf_op jit(solution)/shard_map/pallas_call | solution.py:162
  2.1 33.3 %all_to_all.15.own_ref = bf16[32,96,128]{2,1,0:T(8,128)(2,1)S(1)} all-to-all(bf16[32,96,128]{2,1,0:T(8,128)(2,1)} %shard_map.37), channel_id=1, replica_groups=mesh['z'=8,'x'=4,'y'=8,'core'=2] {'x','y'}, dimensions={0} | all-to-all | bytes 1572864 | tf_op jit(solution)/shard_map/all_to_all | solution.py:175
  35.4 0.9 %broadcast_in_dim.2 = bf16[8,256,128]{2,1,0:T(8,128)(2,1)} broadcast(bf16[256,128]{1,0:T(8,128)(2,1)S(1)} %pad_maximum_fusion.1), dimensions={1,2} | broadcast | bytes 589824 | tf_op jit(solution)/shard_map/broadcast_in_dim | solution.py:186
  36.3 3.9 %all-to-all-start.1 = ((bf16[8,256,128]{2,1,0:T(8,128)(2,1)}), bf16[8,256,128]{2,1,0:T(8,128)(2,1)S(1)}, u32[]{:S(2)}, u32[]{:S(2)}) async-start(bf16[8,256,128]{2,1,0:T(8,128)(2,1)} %broadcast_in_dim.2), calls=%async_computation.1 | async-start | bytes 1048576 | tf_op jit(solution)/shard_map/all_to_all | solution.py:187
  40.2 4.3 %collective-permute-start = (bf16[16,64,128]{2,1,0:T(8,128)(2,1)S(1)}, bf16[16,64,128]{2,1,0:T(8,128)(2,1)S(1)}, u32[]{:S(2)}, u32[]{:S(2)}) collective-permute-start(bf16[16,64,128]{2,1,0:T(8,128)(2,1)S(1)} %slice.17), channel_id=1, source_target_pairs={{0,64},{64,128},{128,192},{192,256},{256,320},{320,384},{384,448},... | collective-permute-start | bytes 786440 | tf_op jit(solution)/shard_map/ppermute | solution.py:179
  44.5 0.1 slice.18
  44.5 3.8 %collective-permute-start.1 = (bf16[32,64,128]{2,1,0:T(8,128)(2,1)S(1)}, bf16[32,64,128]{2,1,0:T(8,128)(2,1)S(1)}, u32[]{:S(2)}, u32[]{:S(2)}) collective-permute-start(bf16[32,64,128]{2,1,0:T(8,128)(2,1)S(1)} %slice.18), channel_id=1, source_target_pairs={{0,1},{1,0},{2,3},{3,2},{4,5},{5,4},{6,7},{7,6},{8,9},{9,8},{10,11... | collective-permute-start | bytes 1572872 | tf_op jit(solution)/shard_map/ppermute | solution.py:180
  48.4 5.7 %collective-permute-done = bf16[16,64,128]{2,1,0:T(8,128)(2,1)S(1)} collective-permute-done((bf16[16,64,128]{2,1,0:T(8,128)(2,1)S(1)}, bf16[16,64,128]{2,1,0:T(8,128)(2,1)S(1)}, u32[]{:S(2)}, u32[]{:S(2)}) %collective-permute-start) | collective-permute-done | bytes 262176 | tf_op jit(solution)/shard_map/ppermute | solution.py:179
  54.0 0.0 all-to-all-done.1
  54.1 0.1 pad_maximum_fusion.late_ref
  54.1 0.0 collective-permute-done.1.other_ref
  54.1 3.5 %collective-permute-start.2 = (bf16[3072,128]{1,0:T(8,128)(2,1)S(1)}, bf16[3072,128]{1,0:T(8,128)(2,1)S(1)}, u32[]{:S(2)}, u32[]{:S(2)}) collective-permute-start(bf16[3072,128]{1,0:T(8,128)(2,1)S(1)} %pad_maximum_fusion.late_ref), channel_id=1, source_target_pairs={{0,1},{1,0},{2,3},{3,2},{4,5},{5,4},{6,7},{7,6},{8,9},{9,8},{10,11... | collective-permute-start | bytes 2359304 | tf_op jit(solution)/shard_map/ppermute | solution.py:190
  57.7 0.1 pad_add_fusion.place_ref
  57.7 2.7 %shard_map.38 = (f32[1024,128]{1,0:T(8,128)S(1)}, f32[1024,128]{1,0:T(8,128)S(1)}, f32[1024,128]{1,0:T(8,128)S(1)}) custom-call(s32[2]{0:T(128)S(1)} %pad_add_fusion.place_ref, bf16[32,96,128]{2,1,0:T(8,128)(2,1)S(1)} %all_to_all.15.own_ref, bf16[32,64,128]{2,1,0:T(8,128)(2,1)S(1)} %collective-permute-done.1.other_ref), custom_call_target="tpu_custom_call" | custom-call | flops 400000000 | bytes 3000000 | tf_op jit(solution)/shard_map/pallas_call | solution.py:194
  60.5 0.0 collective-permute-done.2.late_other_ref
  60.5 2.9 %shard_map.39 = bf16[32,32,128]{2,1,0:T(8,128)(2,1)S(1)} custom-call(s32[2]{0:T(128)S(1)} %pad_add_fusion.place_ref, bf16[32,96,128]{2,1,0:T(8,128)(2,1)S(1)} %all_to_all.15.own_ref, bf16[3072,128]{1,0:T(8,128)(2,1)S(1)} %pad_maximum_fusion.late_ref, bf16[3072,128]{1,0:T(8,128)(2,1)S(1)} %collective-permute-done.2.late_other_ref, ...), custom_call_target="tpu_custom_call" | custom-call | tf_op jit(solution)/shard_map/pallas_call | solution.py:202
  63.4 19.4 %all_to_all.16.in_ref = bf16[32,32,128]{2,1,0:T(8,128)(2,1)S(1)} all-to-all(bf16[32,32,128]{2,1,0:T(8,128)(2,1)S(1)} %shard_map.39), channel_id=1, replica_groups=mesh['z'=8,'x'=4,'y'=8,'core'=2] {'x','y'}, dimensions={0} | all-to-all | bytes 524288 | tf_op jit(solution)/shard_map/all_to_all | solution.py:209
  82.8 0.7 shard_map.40
  (3 shorter events, 0.0 us)
Async XLA Ops:
  36.3 17.8 %all-to-all-start.1 = ((bf16[8,256,128]{2,1,0:T(8,128)(2,1)}), bf16[8,256,128]{2,1,0:T(8,128)(2,1)S(1)}, u32[]{:S(2)}, u32[]{:S(2)}) async-start(bf16[8,256,128]{2,1,0:T(8,128)(2,1)} %broadcast_in_dim.2), calls=%async_computation.1 | async-start | bytes 1048576 | tf_op jit(solution)/shard_map/all_to_all | solution.py:187
  40.2 13.9 %collective-permute-start = (bf16[16,64,128]{2,1,0:T(8,128)(2,1)S(1)}, bf16[16,64,128]{2,1,0:T(8,128)(2,1)S(1)}, u32[]{:S(2)}, u32[]{:S(2)}) collective-permute-start(bf16[16,64,128]{2,1,0:T(8,128)(2,1)S(1)} %slice.17), channel_id=1, source_target_pairs={{0,64},{64,128},{128,192},{192,256},{256,320},{320,384},{384,448},... | collective-permute-start | bytes 786440 | tf_op jit(solution)/shard_map/ppermute | solution.py:179
  44.5 9.6 %collective-permute-start.1 = (bf16[32,64,128]{2,1,0:T(8,128)(2,1)S(1)}, bf16[32,64,128]{2,1,0:T(8,128)(2,1)S(1)}, u32[]{:S(2)}, u32[]{:S(2)}) collective-permute-start(bf16[32,64,128]{2,1,0:T(8,128)(2,1)S(1)} %slice.18), channel_id=1, source_target_pairs={{0,1},{1,0},{2,3},{3,2},{4,5},{5,4},{6,7},{7,6},{8,9},{9,8},{10,11... | collective-permute-start | bytes 1572872 | tf_op jit(solution)/shard_map/ppermute | solution.py:180
  54.1 6.4 %collective-permute-start.2 = (bf16[3072,128]{1,0:T(8,128)(2,1)S(1)}, bf16[3072,128]{1,0:T(8,128)(2,1)S(1)}, u32[]{:S(2)}, u32[]{:S(2)}) collective-permute-start(bf16[3072,128]{1,0:T(8,128)(2,1)S(1)} %pad_maximum_fusion.late_ref), channel_id=1, source_target_pairs={{0,1},{1,0},{2,3},{3,2},{4,5},{5,4},{6,7},{7,6},{8,9},{9,8},{10,11... | collective-permute-start | bytes 2359304 | tf_op jit(solution)/shard_map/ppermute | solution.py:190
